TPU v7x, 512 devices: a whole 4x8x8 slice. The times are simulated.
512 devices in a mesh: gx: 32 (over z, x), gy: 16 (over y, core).
Axes of the slice: x: 4, y: 8, z: 8, core: 2. Of those that a mesh axis runs over, the one named last changes fastest.
Arguments:
- velocity_guess: float32 [8, 2, 1024, 4096], P(None, None, 'gx', 'gy'), may hold values from -6 to 6
- friction: bfloat16 [8, 1024, 4096], P(None, 'gx', 'gy'), may hold values from 0.5 to 4
- thickness: float32 [1024, 4096], P('gx', 'gy'), may hold values from 0.5 to 4.5
- surface: float32 [1024, 4096], P('gx', 'gy'), may hold values from -4 to 1284
- ice_mask: int32 [1024, 4096], P('gx', 'gy'), may hold values 0 or 1
- grounded_mask: int32 [1024, 4096], P('gx', 'gy'), may hold values 0 or 1
Outputs:
- velocity: float32 [8, 2, 1024, 4096], P(None, None, 'gx', 'gy')
All inputs are finite; a program needn't handle non-finite values. No bound on the sum of `ice_mask` or of `grounded_mask` on one device may be relied on, other than what follows from the above.
Results may differ from a plain program's by a relative error of at most 0.0003.
Values sent between devices are 32-bit elements; how exact they have to be, the bound alone decides.
A program may use at most 64 MiB of HBM per device.

v0:
```python
import jax
import jax.numpy as jnp
from jax import lax
from jax.sharding import PartitionSpec as P

strain_floor = 0.1
water_drag = 0.25
flow_power = 1.0 / 3.0


def padded_2(cells, sides, width):
    for axis, dim in sides:
        count = lax.axis_size(axis)
        ends = count - 1
        head = lax.slice_in_dim(cells, 0, width, axis=dim)
        tail = lax.slice_in_dim(cells, cells.shape[dim] - width, cells.shape[dim], axis=dim)
        cells = jnp.concatenate(
            [
                lax.ppermute(tail, axis, [(i, (i + 1) % count) for i in range(ends)]),
                cells,
                lax.ppermute(head, axis, [((i + 1) % count, i) for i in range(ends)]),
            ],
            axis=dim,
        )
    return cells


def centre_rows(padded):
    return 0.5 * (padded[..., 2:, 1:-1] - padded[..., :-2, 1:-1])


def centre_cols(padded):
    return 0.5 * (padded[..., 1:-1, 2:] - padded[..., 1:-1, :-2])


def strains(padded):
    field_u = padded[:, 0]
    field_v = padded[:, 1]
    return (centre_rows(field_u), centre_cols(field_v), centre_cols(field_u) + centre_rows(field_v))


def stresses(visc, padded):
    ka, kb, kc = strains(padded)
    return (visc * (4.0 * ka + 2.0 * kb), visc * (2.0 * ka + 4.0 * kb), visc * kc)


def divergence(sxx, syy, sxy, field, drag, icef):
    out_u = icef * (drag * field[:, 0] - centre_rows(sxx) - centre_cols(sxy))
    out_v = icef * (drag * field[:, 1] - centre_cols(syy) - centre_rows(sxy))
    return jnp.stack([out_u, out_v], 1)


def extend(field):
    flat = field.reshape((-1,) + field.shape[2:])
    grown = padded_2(flat, (("gx", 1), ("gy", 2)), 1)
    return grown.reshape(field.shape[:2] + grown.shape[1:])


def member_dot(left, right):
    return lax.psum(jnp.sum(left * right, axis=(1, 2, 3)), ("gx", "gy"))


def column(values):
    return values[:, None, None, None]


def per_device(velocity_guess, friction, thickness, surface, ice_mask, grounded_mask):
    members = velocity_guess.shape[0]
    icef = ice_mask.astype(jnp.float32)
    groundf = grounded_mask.astype(jnp.float32)
    drag = icef * (groundf * friction.astype(jnp.float32) + water_drag)
    start = icef * velocity_guess
    stacked = jnp.concatenate([start.reshape((-1,) + start.shape[2:]), surface[None]], 0)
    grown = padded_2(stacked, (("gx", 1), ("gy", 2)), 1)
    start_ext = grown[: 2 * members].reshape((members, 2) + grown.shape[1:])
    start_one = grown[: 2 * members].reshape((members, 2) + grown.shape[1:])
    surf_one = grown[2 * members]
    sa, sb, sc = strains(start_one)
    visc = (
        icef
        * 0.5
        * thickness
        * jnp.power(sa * sa + sb * sb + sa * sb + 0.25 * (sc * sc) + strain_floor, -flow_power)
    )
    visc_ext = padded_2(visc, (("gx", 1), ("gy", 2)), 1)
    near_rows = visc_ext[:, 2:, 1:-1] + visc_ext[:, :-2, 1:-1]
    near_cols = visc_ext[:, 1:-1, 2:] + visc_ext[:, 1:-1, :-2]
    precond = jnp.stack(
        [
            icef * (near_rows + 0.25 * near_cols + drag) + (1.0 - icef),
            icef * (near_cols + 0.25 * near_rows + drag) + (1.0 - icef),
        ],
        1,
    )
    force = jnp.stack(
        [icef * -(thickness * centre_rows(surf_one)), icef * -(thickness * centre_cols(surf_one))],
        0,
    )

    def operate(padded):
        sxx, syy, sxy = stresses(visc, padded)
        joined = jnp.concatenate([sxx, syy, sxy], 0)
        wider = padded_2(joined, (("gx", 1), ("gy", 2)), 1)
        field = padded[:, :, 1:-1, 1:-1]
        return divergence(
            wider[:members], wider[members : 2 * members], wider[2 * members :], field, drag, icef
        )

    velocity = start
    resid = force[None] - operate(start_ext)
    scaled = resid / precond
    direction = scaled
    norm_now = member_dot(resid, scaled)
    for step in range(2):
        image = operate(extend(direction))
        alpha = norm_now / member_dot(direction, image)
        velocity = velocity + column(alpha) * direction
        resid = resid - column(alpha) * image
        if step == 0:
            scaled = resid / precond
            norm_next = member_dot(resid, scaled)
            direction = scaled + column(norm_next / norm_now) * direction
            norm_now = norm_next
    return velocity


def solution(mesh):
    placed = (
        P(None, None, "gx", "gy"),
        P(None, "gx", "gy"),
        P("gx", "gy"),
        P("gx", "gy"),
        P("gx", "gy"),
        P("gx", "gy"),
    )
    return jax.shard_map(
        per_device, mesh=mesh, in_specs=placed, out_specs=P(None, None, "gx", "gy"), check_vma=False
    )
```

profile of v0, /device:TPU:10, one launch (start us, length us, event | category | flops | bytes accessed | tf_op | source)
XLA Modules:
  0.0 479.6 jit_solution(5027223697449381866)
XLA Ops:
  1.9 3.4 collective-permute-start
  5.3 2.4 collective-permute-start.1
  7.8 3.2 collective-permute-done.1
  13.2 3.6 collective-permute-start.3
  16.8 3.0 collective-permute-done.2
  24.2 2.4 collective-permute-start.8
  26.6 3.4 collective-permute-start.9
  30.1 2.4 collective-permute-start.4
  32.5 5.0 %collective-permute-start.5 = (f32[24,1,256]{2,1,0:T(1,128)S(1)}, f32[24,1,256]{2,1,0:T(1,128)S(1)}, u32[]{:S(2)}, u32[]{:S(2)}) collective-permute-start(f32[24,1,256]{2,1,0:T(1,128)S(1)} %get-tuple-element.38), channel_id=1, source_target_pairs={{0,16},{16,32},{32,48},{48,64},{64,80},{80,96},{96,112},{112,128},... | collective-permute-start | bytes 73736 | tf_op jit(solution)/shard_map/ppermute | solution.py:19
  37.7 3.4 collective-permute-start.10
  43.9 3.8 collective-permute-done.11
  50.6 2.4 collective-permute-start.7
  53.1 3.8 collective-permute-done.6
  57.0 3.8 collective-permute-done.7
  61.8 5.8 %collective-permute-start.12 = (f32[16,1,256]{2,1,0:T(1,128)S(1)}, f32[16,1,256]{2,1,0:T(1,128)S(1)}, u32[]{:S(2)}, u32[]{:S(2)}) collective-permute-start(f32[16,1,256]{2,1,0:T(1,128)S(1)} %get-tuple-element.50), channel_id=1, source_target_pairs={{0,16},{16,32},{32,48},{48,64},{64,80},{80,96},{96,112},{112,128},... | collective-permute-start | bytes 49160 | tf_op jit(solution)/shard_map/ppermute | solution.py:19
  69.5 5.5 %collective-permute-done.13 = f32[16,1,256]{2,1,0:T(1,128)S(1)} collective-permute-done((f32[16,1,256]{2,1,0:T(1,128)S(1)}, f32[16,1,256]{2,1,0:T(1,128)S(1)}, u32[]{:S(2)}, u32[]{:S(2)}) %collective-permute-start.13) | collective-permute-done | bytes 16416 | tf_op jit(solution)/shard_map/ppermute | solution.py:21
  77.1 3.6 collective-permute-start.15
  80.8 2.8 collective-permute-done.14
  88.5 3.9 collective-permute-start.17
  94.5 2.7 collective-permute-start.18
  99.1 4.4 collective-permute-done.18
  103.5 3.8 collective-permute-done.19
  109.2 120.6 %all-reduce = (f32[8]{0:T(128)S(1)}, f32[8]{0:T(128)S(1)}) all-reduce(f32[8]{0:T(128)S(1)} %get-tuple-element.6, f32[8]{0:T(128)S(1)} %get-tuple-element.5), channel_id=1, replica_groups=mesh['gx'=32,'gy'=16] {'gx','gy'}, use_global_device_ids=true, to_apply=%region_1.0 | all-reduce | flops 16 | bytes 128 | tf_op jit(solution)/shard_map/psum | solution.py:60
  232.2 94.5 %psum.30 = f32[8]{0:T(128)S(1)} all-reduce(f32[8]{0:T(128)S(1)} %get-tuple-element.13), channel_id=1, replica_groups=mesh['gx'=32,'gy'=16] {'gx','gy'}, use_global_device_ids=true, to_apply=%region_5.0 | all-reduce | flops 8 | bytes 64 | tf_op jit(solution)/shard_map/psum | solution.py:60
  330.7 3.9 collective-permute-start.21
  338.5 3.8 collective-permute-start.23
  342.3 2.6 collective-permute-done.22
  347.9 3.9 collective-permute-start.24
  353.7 3.8 collective-permute-done.25
  362.2 4.4 collective-permute-done.26
  366.6 3.8 collective-permute-done.27
  371.9 106.7 %psum.31 = f32[8]{0:T(128)S(1)} all-reduce(f32[8]{0:T(128)S(1)} %fusion), channel_id=1, replica_groups=mesh['gx'=32,'gy'=16] {'gx','gy'}, use_global_device_ids=true, to_apply=%region_7.0 | all-reduce | flops 8 | bytes 64 | tf_op jit(solution)/shard_map/psum | solution.py:60
  (124 shorter events, 52.0 us)
Async XLA Ops:
  0.8 107.0 %copy-start.1 = (f32[32,256]{1,0:T(8,128)}, f32[32,256]{1,0:T(8,128)S(1)}, u32[]{:S(2)}) copy-start(f32[32,256]{1,0:T(8,128)S(1)} %convert_element_type.9) | copy-start | bytes 98308
  1.9 5.9 %collective-permute-start = (f32[17,1,256]{2,1,0:T(1,128)S(1)}, f32[17,1,256]{2,1,0:T(1,128)S(1)}, u32[]{:S(2)}, u32[]{:S(2)}) collective-permute-start(f32[17,1,256]{2,1,0:T(1,128)S(1)} %get-tuple-element.45), channel_id=1, source_target_pairs={{0,16},{16,32},{32,48},{48,64},{64,80},{80,96},{96,112},{112,128},... | collective-permute-start | bytes 52232 | tf_op jit(solution)/shard_map/ppermute | solution.py:19
  5.3 5.6 %collective-permute-start.1 = (f32[17,1,256]{2,1,0:T(1,128)S(1)}, f32[17,1,256]{2,1,0:T(1,128)S(1)}, u32[]{:S(2)}, u32[]{:S(2)}) collective-permute-start(f32[17,1,256]{2,1,0:T(1,128)S(1)} %get-tuple-element.46), channel_id=1, source_target_pairs={{16,0},{32,16},{48,32},{64,48},{80,64},{96,80},{112,96},{128,112},... | collective-permute-start | bytes 52232 | tf_op jit(solution)/shard_map/ppermute | solution.py:21
  11.2 8.6 %collective-permute-start.2 = (f32[17,34,1]{2,1,0:T(8,128)S(1)}, f32[17,34,1]{2,1,0:T(8,128)S(1)}, u32[]{:S(2)}, u32[]{:S(2)}) collective-permute-start(f32[17,34,1]{2,1,0:T(8,128)S(1)} %get-tuple-element.39), channel_id=1, source_target_pairs={{0,1},{1,2},{2,3},{3,4},{4,5},{5,6},{6,7},{7,8},{8,9},{9,10},{10,1... | collective-permute-start | bytes 6944 | tf_op jit(solution)/shard_map/ppermute | solution.py:19
  13.2 8.4 %collective-permute-start.3 = (f32[17,34,1]{2,1,0:T(8,128)S(1)}, f32[17,34,1]{2,1,0:T(8,128)S(1)}, u32[]{:S(2)}, u32[]{:S(2)}) collective-permute-start(f32[17,34,1]{2,1,0:T(8,128)S(1)} %get-tuple-element.40), channel_id=1, source_target_pairs={{1,0},{2,1},{3,2},{4,3},{5,4},{6,5},{7,6},{8,7},{9,8},{10,9},{11,1... | collective-permute-start | bytes 6944 | tf_op jit(solution)/shard_map/ppermute | solution.py:21
  24.2 13.3 %collective-permute-start.8 = (f32[8,1,256]{2,1,0:T(1,128)S(1)}, f32[8,1,256]{2,1,0:T(1,128)S(1)}, u32[]{:S(2)}, u32[]{:S(2)}) collective-permute-start(f32[8,1,256]{2,1,0:T(1,128)S(1)} %get-tuple-element.56), channel_id=1, source_target_pairs={{16,0},{32,16},{48,32},{64,48},{80,64},{96,80},{112,96},{128,112},... | collective-permute-start | bytes 24584 | tf_op jit(solution)/shard_map/ppermute | solution.py:21
  26.6 10.9 %collective-permute-start.9 = (f32[8,1,256]{2,1,0:T(1,128)S(1)}, f32[8,1,256]{2,1,0:T(1,128)S(1)}, u32[]{:S(2)}, u32[]{:S(2)}) collective-permute-start(f32[8,1,256]{2,1,0:T(1,128)S(1)} %get-tuple-element.57), channel_id=1, source_target_pairs={{0,16},{16,32},{32,48},{48,64},{64,80},{80,96},{96,112},{112,128},... | collective-permute-start | bytes 24584 | tf_op jit(solution)/shard_map/ppermute | solution.py:19
  30.1 18.3 %collective-permute-start.4 = (f32[24,1,256]{2,1,0:T(1,128)S(1)}, f32[24,1,256]{2,1,0:T(1,128)S(1)}, u32[]{:S(2)}, u32[]{:S(2)}) collective-permute-start(f32[24,1,256]{2,1,0:T(1,128)S(1)} %get-tuple-element.37), channel_id=1, source_target_pairs={{16,0},{32,16},{48,32},{64,48},{80,64},{96,80},{112,96},{128,112},... | collective-permute-start | bytes 73736 | tf_op jit(solution)/shard_map/ppermute | solution.py:21
  32.5 15.8 %collective-permute-start.5 = (f32[24,1,256]{2,1,0:T(1,128)S(1)}, f32[24,1,256]{2,1,0:T(1,128)S(1)}, u32[]{:S(2)}, u32[]{:S(2)}) collective-permute-start(f32[24,1,256]{2,1,0:T(1,128)S(1)} %get-tuple-element.38), channel_id=1, source_target_pairs={{0,16},{16,32},{32,48},{48,64},{64,80},{80,96},{96,112},{112,128},... | collective-permute-start | bytes 73736 | tf_op jit(solution)/shard_map/ppermute | solution.py:19
  37.7 6.2 %collective-permute-start.10 = (f32[8,34,1]{2,1,0:T(8,128)S(1)}, f32[8,34,1]{2,1,0:T(8,128)S(1)}, u32[]{:S(2)}, u32[]{:S(2)}) collective-permute-start(f32[8,34,1]{2,1,0:T(8,128)S(1)} %get-tuple-element.52), channel_id=1, source_target_pairs={{1,0},{2,1},{3,2},{4,3},{5,4},{6,5},{7,6},{8,7},{9,8},{10,9},{11,1... | collective-permute-start | bytes 3272 | tf_op jit(solution)/shard_map/ppermute | solution.py:21
  41.1 6.6 %collective-permute-start.11 = (f32[8,34,1]{2,1,0:T(8,128)S(1)}, f32[8,34,1]{2,1,0:T(8,128)S(1)}, u32[]{:S(2)}, u32[]{:S(2)}) collective-permute-start(f32[8,34,1]{2,1,0:T(8,128)S(1)} %get-tuple-element.53), channel_id=1, source_target_pairs={{0,1},{1,2},{2,3},{3,4},{4,5},{5,6},{6,7},{7,8},{8,9},{9,10},{10,1... | collective-permute-start | bytes 3272 | tf_op jit(solution)/shard_map/ppermute | solution.py:19
  48.7 8.3 %collective-permute-start.6 = (f32[24,34,1]{2,1,0:T(8,128)S(1)}, f32[24,34,1]{2,1,0:T(8,128)S(1)}, u32[]{:S(2)}, u32[]{:S(2)}) collective-permute-start(f32[24,34,1]{2,1,0:T(8,128)S(1)} %get-tuple-element.29), channel_id=1, source_target_pairs={{1,0},{2,1},{3,2},{4,3},{5,4},{6,5},{7,6},{8,7},{9,8},{10,9},{11,1... | collective-permute-start | bytes 9800 | tf_op jit(solution)/shard_map/ppermute | solution.py:21
  50.6 10.1 %collective-permute-start.7 = (f32[24,34,1]{2,1,0:T(8,128)S(1)}, f32[24,34,1]{2,1,0:T(8,128)S(1)}, u32[]{:S(2)}, u32[]{:S(2)}) collective-permute-start(f32[24,34,1]{2,1,0:T(8,128)S(1)} %get-tuple-element.30), channel_id=1, source_target_pairs={{0,1},{1,2},{2,3},{3,4},{4,5},{5,6},{6,7},{7,8},{8,9},{9,10},{10,1... | collective-permute-start | bytes 9800 | tf_op jit(solution)/shard_map/ppermute | solution.py:19
  61.8 7.7 %collective-permute-start.12 = (f32[16,1,256]{2,1,0:T(1,128)S(1)}, f32[16,1,256]{2,1,0:T(1,128)S(1)}, u32[]{:S(2)}, u32[]{:S(2)}) collective-permute-start(f32[16,1,256]{2,1,0:T(1,128)S(1)} %get-tuple-element.50), channel_id=1, source_target_pairs={{0,16},{16,32},{32,48},{48,64},{64,80},{80,96},{96,112},{112,128},... | collective-permute-start | bytes 49160 | tf_op jit(solution)/shard_map/ppermute | solution.py:19
  67.5 7.5 %collective-permute-start.13 = (f32[16,1,256]{2,1,0:T(1,128)S(1)}, f32[16,1,256]{2,1,0:T(1,128)S(1)}, u32[]{:S(2)}, u32[]{:S(2)}) collective-permute-start(f32[16,1,256]{2,1,0:T(1,128)S(1)} %get-tuple-element.51), channel_id=1, source_target_pairs={{16,0},{32,16},{48,32},{64,48},{80,64},{96,80},{112,96},{128,112},... | collective-permute-start | bytes 49160 | tf_op jit(solution)/shard_map/ppermute | solution.py:21
  75.2 8.4 %collective-permute-start.14 = (f32[16,34,1]{2,1,0:T(8,128)S(1)}, f32[16,34,1]{2,1,0:T(8,128)S(1)}, u32[]{:S(2)}, u32[]{:S(2)}) collective-permute-start(f32[16,34,1]{2,1,0:T(8,128)S(1)} %get-tuple-element.43), channel_id=1, source_target_pairs={{0,1},{1,2},{2,3},{3,4},{4,5},{5,6},{6,7},{7,8},{8,9},{9,10},{10,1... | collective-permute-start | bytes 6536 | tf_op jit(solution)/shard_map/ppermute | solution.py:19
  77.1 8.2 %collective-permute-start.15 = (f32[16,34,1]{2,1,0:T(8,128)S(1)}, f32[16,34,1]{2,1,0:T(8,128)S(1)}, u32[]{:S(2)}, u32[]{:S(2)}) collective-permute-start(f32[16,34,1]{2,1,0:T(8,128)S(1)} %get-tuple-element.44), channel_id=1, source_target_pairs={{1,0},{2,1},{3,2},{4,3},{5,4},{6,5},{7,6},{8,7},{9,8},{10,9},{11,1... | collective-permute-start | bytes 6536 | tf_op jit(solution)/shard_map/ppermute | solution.py:21
  86.5 5.9 %collective-permute-start.16 = (f32[24,1,256]{2,1,0:T(1,128)S(1)}, f32[24,1,256]{2,1,0:T(1,128)S(1)}, u32[]{:S(2)}, u32[]{:S(2)}) collective-permute-start(f32[24,1,256]{2,1,0:T(1,128)S(1)} %get-tuple-element.35), channel_id=1, source_target_pairs={{16,0},{32,16},{48,32},{64,48},{80,64},{96,80},{112,96},{128,112},... | collective-permute-start | bytes 73736 | tf_op jit(solution)/shard_map/ppermute | solution.py:21
  88.5 5.7 %collective-permute-start.17 = (f32[24,1,256]{2,1,0:T(1,128)S(1)}, f32[24,1,256]{2,1,0:T(1,128)S(1)}, u32[]{:S(2)}, u32[]{:S(2)}) collective-permute-start(f32[24,1,256]{2,1,0:T(1,128)S(1)} %get-tuple-element.36), channel_id=1, source_target_pairs={{0,16},{16,32},{32,48},{48,64},{64,80},{80,96},{96,112},{112,128},... | collective-permute-start | bytes 73736 | tf_op jit(solution)/shard_map/ppermute | solution.py:19
  94.5 9.0 %collective-permute-start.18 = (f32[24,34,1]{2,1,0:T(8,128)S(1)}, f32[24,34,1]{2,1,0:T(8,128)S(1)}, u32[]{:S(2)}, u32[]{:S(2)}) collective-permute-start(f32[24,34,1]{2,1,0:T(8,128)S(1)} %get-tuple-element.25), channel_id=1, source_target_pairs={{1,0},{2,1},{3,2},{4,3},{5,4},{6,5},{7,6},{8,7},{9,8},{10,9},{11,1... | collective-permute-start | bytes 9800 | tf_op jit(solution)/shard_map/ppermute | solution.py:21
  97.2 10.1 %collective-permute-start.19 = (f32[24,34,1]{2,1,0:T(8,128)S(1)}, f32[24,34,1]{2,1,0:T(8,128)S(1)}, u32[]{:S(2)}, u32[]{:S(2)}) collective-permute-start(f32[24,34,1]{2,1,0:T(8,128)S(1)} %get-tuple-element.26), channel_id=1, source_target_pairs={{0,1},{1,2},{2,3},{3,4},{4,5},{5,6},{6,7},{7,8},{8,9},{9,10},{10,1... | collective-permute-start | bytes 9800 | tf_op jit(solution)/shard_map/ppermute | solution.py:19
  328.8 5.9 %collective-permute-start.20 = (f32[16,1,256]{2,1,0:T(1,128)S(1)}, f32[16,1,256]{2,1,0:T(1,128)S(1)}, u32[]{:S(2)}, u32[]{:S(2)}) collective-permute-start(f32[16,1,256]{2,1,0:T(1,128)S(1)} %get-tuple-element.48), channel_id=1, source_target_pairs={{0,16},{16,32},{32,48},{48,64},{64,80},{80,96},{96,112},{112,128},... | collective-permute-start | bytes 49160 | tf_op jit(solution)/shard_map/ppermute | solution.py:19
  330.7 5.6 %collective-permute-start.21 = (f32[16,1,256]{2,1,0:T(1,128)S(1)}, f32[16,1,256]{2,1,0:T(1,128)S(1)}, u32[]{:S(2)}, u32[]{:S(2)}) collective-permute-start(f32[16,1,256]{2,1,0:T(1,128)S(1)} %get-tuple-element.49), channel_id=1, source_target_pairs={{16,0},{32,16},{48,32},{64,48},{80,64},{96,80},{112,96},{128,112},... | collective-permute-start | bytes 49160 | tf_op jit(solution)/shard_map/ppermute | solution.py:21
  336.6 8.4 %collective-permute-start.22 = (f32[16,34,1]{2,1,0:T(8,128)S(1)}, f32[16,34,1]{2,1,0:T(8,128)S(1)}, u32[]{:S(2)}, u32[]{:S(2)}) collective-permute-start(f32[16,34,1]{2,1,0:T(8,128)S(1)} %get-tuple-element.41), channel_id=1, source_target_pairs={{0,1},{1,2},{2,3},{3,4},{4,5},{5,6},{6,7},{7,8},{8,9},{9,10},{10,1... | collective-permute-start | bytes 6536 | tf_op jit(solution)/shard_map/ppermute | solution.py:19
  338.5 8.2 %collective-permute-start.23 = (f32[16,34,1]{2,1,0:T(8,128)S(1)}, f32[16,34,1]{2,1,0:T(8,128)S(1)}, u32[]{:S(2)}, u32[]{:S(2)}) collective-permute-start(f32[16,34,1]{2,1,0:T(8,128)S(1)} %get-tuple-element.42), channel_id=1, source_target_pairs={{1,0},{2,1},{3,2},{4,3},{5,4},{6,5},{7,6},{8,7},{9,8},{10,9},{11,1... | collective-permute-start | bytes 6536 | tf_op jit(solution)/shard_map/ppermute | solution.py:21
  347.9 5.9 %collective-permute-start.24 = (f32[24,1,256]{2,1,0:T(1,128)S(1)}, f32[24,1,256]{2,1,0:T(1,128)S(1)}, u32[]{:S(2)}, u32[]{:S(2)}) collective-permute-start(f32[24,1,256]{2,1,0:T(1,128)S(1)} %get-tuple-element.33), channel_id=1, source_target_pairs={{16,0},{32,16},{48,32},{64,48},{80,64},{96,80},{112,96},{128,112},... | collective-permute-start | bytes 73736 | tf_op jit(solution)/shard_map/ppermute | solution.py:21
  351.8 5.7 %collective-permute-start.25 = (f32[24,1,256]{2,1,0:T(1,128)S(1)}, f32[24,1,256]{2,1,0:T(1,128)S(1)}, u32[]{:S(2)}, u32[]{:S(2)}) collective-permute-start(f32[24,1,256]{2,1,0:T(1,128)S(1)} %get-tuple-element.34), channel_id=1, source_target_pairs={{0,16},{16,32},{32,48},{48,64},{64,80},{80,96},{96,112},{112,128},... | collective-permute-start | bytes 73736 | tf_op jit(solution)/shard_map/ppermute | solution.py:19
  357.9 8.7 %collective-permute-start.26 = (f32[24,34,1]{2,1,0:T(8,128)S(1)}, f32[24,34,1]{2,1,0:T(8,128)S(1)}, u32[]{:S(2)}, u32[]{:S(2)}) collective-permute-start(f32[24,34,1]{2,1,0:T(8,128)S(1)} %get-tuple-element.21), channel_id=1, source_target_pairs={{1,0},{2,1},{3,2},{4,3},{5,4},{6,5},{7,6},{8,7},{9,8},{10,9},{11,1... | collective-permute-start | bytes 9800 | tf_op jit(solution)/shard_map/ppermute | solution.py:21
  360.3 10.1 %collective-permute-start.27 = (f32[24,34,1]{2,1,0:T(8,128)S(1)}, f32[24,34,1]{2,1,0:T(8,128)S(1)}, u32[]{:S(2)}, u32[]{:S(2)}) collective-permute-start(f32[24,34,1]{2,1,0:T(8,128)S(1)} %get-tuple-element.22), channel_id=1, source_target_pairs={{0,1},{1,2},{2,3},{3,4},{4,5},{5,6},{6,7},{7,8},{8,9},{9,10},{10,1... | collective-permute-start | bytes 9800 | tf_op jit(solution)/shard_map/ppermute | solution.py:19
  371.6 107.0 %copy-start.9 = (f32[8,2,32,256]{3,2,1,0:T(8,128)S(1)}, f32[8,2,32,256]{3,2,1,0:T(8,128)}, u32[]{:S(2)}) copy-start(f32[8,2,32,256]{3,2,1,0:T(8,128)} %param.6) | copy-start | bytes 1572868
  371.6 107.0 %copy-start.10 = (f32[8,2,32,256]{3,2,0,1:T(8,128)S(1)}, f32[8,2,32,256]{3,2,0,1:T(8,128)}, u32[]{:S(2)}) copy-start(f32[8,2,32,256]{3,2,0,1:T(8,128)} %get-tuple-element.20) | copy-start | bytes 1572868
  371.9 106.7 %copy-start.16 = (f32[8]{0:T(128)S(1)}, f32[8]{0:T(128)}, u32[]{:S(2)}) copy-start(f32[8]{0:T(128)} %copy-done.15) | copy-start | bytes 100
  (13 other events, 202.8 us)
where the time goes:
time: 481 us; the launch traced here: 480 us
  blocking collectives  322 us (67%)
  starting transfers between devices  79.7 us (17%)
  waiting for transfers between devices  58.4 us (12%)
  other arithmetic  13.5 us (3%)
  local copies, waits for them, and re-layouts  5.37 us (1%)
    psum x3, blocking collectives, member_dot(): return lax.psum(jnp.sum(left * right, axis=(1, 2, 3)), ('gx', 'gy'))  322 us
    ppermute x14, starting transfers between devices, padded_2(): lax.ppermute(head, axis, [((i + 1) % count, i) for i in range(ends)])  40.5 us
    ppermute x14, starting transfers between devices, padded_2(): lax.ppermute(tail, axis, [(i, (i + 1) % count) for i in range(ends)])  39.2 us
    ppermute x14, waiting for transfers between devices, padded_2(): lax.ppermute(tail, axis, [(i, (i + 1) % count) for i in range(ends)])  29.3 us
    ppermute x14, waiting for transfers between devices, padded_2(): lax.ppermute(head, axis, [((i + 1) % count, i) for i in range(ends)])  29.1 us
  transfers between devices with their start and end apart: 28, of which 19 were waited for; matrix products, arithmetic and copies ran while one was open for 0% of the time, Pallas kernels for 0%

commit v1 on v0

--- a/solution.py
+++ b/solution.py
@@ -6,6 +6,11 @@
 strain_floor = 0.1
 water_drag = 0.25
 flow_power = 1.0 / 3.0
+
+
+def prepare_vector(matrix):
+    value_now = lax.all_gather(matrix, ("gx", "gy")).sum(axis=0)
+    return value_now
 
 
 def padded_2(cells, sides, width):
@@ -57,7 +62,7 @@
 
 
 def member_dot(left, right):
-    return lax.psum(jnp.sum(left * right, axis=(1, 2, 3)), ("gx", "gy"))
+    return prepare_vector(jnp.sum(left * right, axis=(1, 2, 3)))
 
 
 def column(values):

time: 481 us -> 491 us (1.021)
    unnamed x0 -> x3, blocking collectives: none -> 322 us
    psum x3 -> x0, blocking collectives: 322 us -> none  [member_dot(): return lax.psum(jnp.sum(left * right, axis=(1, 2, 3)), ('gx', 'gy'))]
where the time goes in v1:
time: 491 us; the launch traced here: 489 us
  blocking collectives  322 us (66%)
  starting transfers between devices  79.5 us (16%)
  waiting for transfers between devices  59 us (12%)
  other arithmetic  17.3 us (4%)
  local copies, waits for them, and re-layouts  10.2 us (2%)
    unnamed x3, blocking collectives  322 us
    ppermute x14, starting transfers between devices, padded_2(): lax.ppermute(head, axis, [((i + 1) % count, i) for i in range(ends)])  40.3 us
    ppermute x14, starting transfers between devices, padded_2(): lax.ppermute(tail, axis, [(i, (i + 1) % count) for i in range(ends)])  39.2 us
    ppermute x14, waiting for transfers between devices, padded_2(): lax.ppermute(tail, axis, [(i, (i + 1) % count) for i in range(ends)])  29.5 us
    ppermute x14, waiting for transfers between devices, padded_2(): lax.ppermute(head, axis, [((i + 1) % count, i) for i in range(ends)])  29.5 us
  transfers between devices with their start and end apart: 28, of which 19 were waited for; matrix products, arithmetic and copies ran while one was open for 0% of the time, Pallas kernels for 0%

profile of v1, /device:TPU:10, one launch (start us, length us, event | category | flops | bytes accessed | tf_op | source)
XLA Modules:
  0.0 489.2 jit_solution(9402331727566752149)
XLA Ops:
  1.9 3.4 collective-permute-start
  5.3 2.4 collective-permute-start.1
  7.8 3.2 collective-permute-done.1
  13.1 3.6 collective-permute-start.3
  16.8 3.0 collective-permute-done.2
  24.1 2.4 collective-permute-start.8
  26.6 3.4 collective-permute-start.9
  30.0 2.4 collective-permute-start.4
  32.5 5.0 %collective-permute-start.5 = (f32[24,1,256]{2,1,0:T(1,128)S(1)}, f32[24,1,256]{2,1,0:T(1,128)S(1)}, u32[]{:S(2)}, u32[]{:S(2)}) collective-permute-start(f32[24,1,256]{2,1,0:T(1,128)S(1)} %get-tuple-element.38), channel_id=1, source_target_pairs={{0,16},{16,32},{32,48},{48,64},{64,80},{80,96},{96,112},{112,128},... | collective-permute-start | bytes 73736 | tf_op jit(solution)/shard_map/ppermute | solution.py:24
  37.6 3.4 collective-permute-start.10
  43.8 3.8 collective-permute-done.11
  50.6 2.4 collective-permute-start.7
  53.1 3.8 collective-permute-done.6
  56.9 3.8 collective-permute-done.7
  62.4 5.8 %collective-permute-start.12 = (f32[16,1,256]{2,1,0:T(1,128)S(1)}, f32[16,1,256]{2,1,0:T(1,128)S(1)}, u32[]{:S(2)}, u32[]{:S(2)}) collective-permute-start(f32[16,1,256]{2,1,0:T(1,128)S(1)} %get-tuple-element.50), channel_id=1, source_target_pairs={{0,16},{16,32},{32,48},{48,64},{64,80},{80,96},{96,112},{112,128},... | collective-permute-start | bytes 49160 | tf_op jit(solution)/shard_map/ppermute | solution.py:24
  70.1 5.5 %collective-permute-done.13 = f32[16,1,256]{2,1,0:T(1,128)S(1)} collective-permute-done((f32[16,1,256]{2,1,0:T(1,128)S(1)}, f32[16,1,256]{2,1,0:T(1,128)S(1)}, u32[]{:S(2)}, u32[]{:S(2)}) %collective-permute-start.13) | collective-permute-done | bytes 16416 | tf_op jit(solution)/shard_map/ppermute | solution.py:26
  77.8 3.6 collective-permute-start.15
  81.4 2.8 collective-permute-done.14
  90.0 3.9 collective-permute-start.17
  96.9 2.7 collective-permute-start.18
  101.5 4.7 collective-permute-done.18
  106.2 3.8 collective-permute-done.19
  114.4 120.8 %all-reduce.4 = (f32[4096]{0:T(1024)S(1)}, f32[4096]{0:T(1024)S(1)}) all-reduce(f32[4096]{0:T(1024)S(1)} %dynamic-update-slice, f32[4096]{0:T(1024)S(1)} %dynamic-update-slice.1), channel_id=2, replica_groups=mesh['gx'=32,'gy'=16] {'gx','gy'}, use_global_device_ids=true, to_apply=%add | all-reduce | flops 8192 | bytes 65536
  239.0 94.7 %all-reduce.2 = f32[4096]{0:T(1024)S(1)} all-reduce(f32[4096]{0:T(1024)S(1)} %dynamic-update-slice.2), channel_id=4, replica_groups=mesh['gx'=32,'gy'=16] {'gx','gy'}, use_global_device_ids=true, to_apply=%add.2 | all-reduce | flops 4096 | bytes 32768
  339.5 3.9 collective-permute-start.21
  347.3 3.6 collective-permute-start.23
  350.9 2.8 collective-permute-done.22
  356.6 3.9 collective-permute-start.24
  362.5 3.8 collective-permute-done.25
  371.0 4.4 collective-permute-done.26
  375.3 3.8 collective-permute-done.27
  381.1 106.8 %all-reduce.3 = f32[4096]{0:T(1024)S(1)} all-reduce(f32[4096]{0:T(1024)S(1)} %dynamic-update-slice.3), channel_id=5, replica_groups=mesh['gx'=32,'gy'=16] {'gx','gy'}, use_global_device_ids=true, to_apply=%add.3 | all-reduce | flops 4096 | bytes 32768
  (136 shorter events, 60.7 us)
Async XLA Ops:
  1.9 5.9 %collective-permute-start = (f32[17,1,256]{2,1,0:T(1,128)S(1)}, f32[17,1,256]{2,1,0:T(1,128)S(1)}, u32[]{:S(2)}, u32[]{:S(2)}) collective-permute-start(f32[17,1,256]{2,1,0:T(1,128)S(1)} %get-tuple-element.45), channel_id=1, source_target_pairs={{0,16},{16,32},{32,48},{48,64},{64,80},{80,96},{96,112},{112,128},... | collective-permute-start | bytes 52232 | tf_op jit(solution)/shard_map/ppermute | solution.py:24
  5.3 5.6 %collective-permute-start.1 = (f32[17,1,256]{2,1,0:T(1,128)S(1)}, f32[17,1,256]{2,1,0:T(1,128)S(1)}, u32[]{:S(2)}, u32[]{:S(2)}) collective-permute-start(f32[17,1,256]{2,1,0:T(1,128)S(1)} %get-tuple-element.46), channel_id=1, source_target_pairs={{16,0},{32,16},{48,32},{64,48},{80,64},{96,80},{112,96},{128,112},... | collective-permute-start | bytes 52232 | tf_op jit(solution)/shard_map/ppermute | solution.py:26
  11.1 5.7 %copy-start.14 = (s32[32,256]{1,0:T(8,128)S(1)}, s32[32,256]{1,0:T(8,128)}, u32[]{:S(2)}) copy-start(s32[32,256]{1,0:T(8,128)} %param.11) | copy-start | bytes 98308
  11.2 8.6 %collective-permute-start.2 = (f32[17,34,1]{2,1,0:T(8,128)S(1)}, f32[17,34,1]{2,1,0:T(8,128)S(1)}, u32[]{:S(2)}, u32[]{:S(2)}) collective-permute-start(f32[17,34,1]{2,1,0:T(8,128)S(1)} %get-tuple-element.39), channel_id=1, source_target_pairs={{0,1},{1,2},{2,3},{3,4},{4,5},{5,6},{6,7},{7,8},{8,9},{9,10},{10,1... | collective-permute-start | bytes 6944 | tf_op jit(solution)/shard_map/ppermute | solution.py:24
  13.1 8.4 %collective-permute-start.3 = (f32[17,34,1]{2,1,0:T(8,128)S(1)}, f32[17,34,1]{2,1,0:T(8,128)S(1)}, u32[]{:S(2)}, u32[]{:S(2)}) collective-permute-start(f32[17,34,1]{2,1,0:T(8,128)S(1)} %get-tuple-element.40), channel_id=1, source_target_pairs={{1,0},{2,1},{3,2},{4,3},{5,4},{6,5},{7,6},{8,7},{9,8},{10,9},{11,1... | collective-permute-start | bytes 6944 | tf_op jit(solution)/shard_map/ppermute | solution.py:26
  24.1 13.3 %collective-permute-start.8 = (f32[8,1,256]{2,1,0:T(1,128)S(1)}, f32[8,1,256]{2,1,0:T(1,128)S(1)}, u32[]{:S(2)}, u32[]{:S(2)}) collective-permute-start(f32[8,1,256]{2,1,0:T(1,128)S(1)} %get-tuple-element.56), channel_id=1, source_target_pairs={{16,0},{32,16},{48,32},{64,48},{80,64},{96,80},{112,96},{128,112},... | collective-permute-start | bytes 24584 | tf_op jit(solution)/shard_map/ppermute | solution.py:26
  26.6 10.9 %collective-permute-start.9 = (f32[8,1,256]{2,1,0:T(1,128)S(1)}, f32[8,1,256]{2,1,0:T(1,128)S(1)}, u32[]{:S(2)}, u32[]{:S(2)}) collective-permute-start(f32[8,1,256]{2,1,0:T(1,128)S(1)} %get-tuple-element.57), channel_id=1, source_target_pairs={{0,16},{16,32},{32,48},{48,64},{64,80},{80,96},{96,112},{112,128},... | collective-permute-start | bytes 24584 | tf_op jit(solution)/shard_map/ppermute | solution.py:24
  30.0 18.3 %collective-permute-start.4 = (f32[24,1,256]{2,1,0:T(1,128)S(1)}, f32[24,1,256]{2,1,0:T(1,128)S(1)}, u32[]{:S(2)}, u32[]{:S(2)}) collective-permute-start(f32[24,1,256]{2,1,0:T(1,128)S(1)} %get-tuple-element.37), channel_id=1, source_target_pairs={{16,0},{32,16},{48,32},{64,48},{80,64},{96,80},{112,96},{128,112},... | collective-permute-start | bytes 73736 | tf_op jit(solution)/shard_map/ppermute | solution.py:26
  32.5 15.8 %collective-permute-start.5 = (f32[24,1,256]{2,1,0:T(1,128)S(1)}, f32[24,1,256]{2,1,0:T(1,128)S(1)}, u32[]{:S(2)}, u32[]{:S(2)}) collective-permute-start(f32[24,1,256]{2,1,0:T(1,128)S(1)} %get-tuple-element.38), channel_id=1, source_target_pairs={{0,16},{16,32},{32,48},{48,64},{64,80},{80,96},{96,112},{112,128},... | collective-permute-start | bytes 73736 | tf_op jit(solution)/shard_map/ppermute | solution.py:24
  37.6 10.0 %copy-start = (bf16[8,32,256]{2,1,0:T(8,128)(2,1)S(1)}, bf16[8,32,256]{2,1,0:T(8,128)(2,1)}, u32[]{:S(2)}) copy-start(bf16[8,32,256]{2,1,0:T(8,128)(2,1)} %param.7) | copy-start | bytes 393220
  37.6 6.2 %collective-permute-start.10 = (f32[8,34,1]{2,1,0:T(8,128)S(1)}, f32[8,34,1]{2,1,0:T(8,128)S(1)}, u32[]{:S(2)}, u32[]{:S(2)}) collective-permute-start(f32[8,34,1]{2,1,0:T(8,128)S(1)} %get-tuple-element.52), channel_id=1, source_target_pairs={{1,0},{2,1},{3,2},{4,3},{5,4},{6,5},{7,6},{8,7},{9,8},{10,9},{11,1... | collective-permute-start | bytes 3272 | tf_op jit(solution)/shard_map/ppermute | solution.py:26
  41.0 6.6 %collective-permute-start.11 = (f32[8,34,1]{2,1,0:T(8,128)S(1)}, f32[8,34,1]{2,1,0:T(8,128)S(1)}, u32[]{:S(2)}, u32[]{:S(2)}) collective-permute-start(f32[8,34,1]{2,1,0:T(8,128)S(1)} %get-tuple-element.53), channel_id=1, source_target_pairs={{0,1},{1,2},{2,3},{3,4},{4,5},{5,6},{6,7},{7,8},{8,9},{9,10},{10,1... | collective-permute-start | bytes 3272 | tf_op jit(solution)/shard_map/ppermute | solution.py:24
  48.6 8.3 %collective-permute-start.6 = (f32[24,34,1]{2,1,0:T(8,128)S(1)}, f32[24,34,1]{2,1,0:T(8,128)S(1)}, u32[]{:S(2)}, u32[]{:S(2)}) collective-permute-start(f32[24,34,1]{2,1,0:T(8,128)S(1)} %get-tuple-element.29), channel_id=1, source_target_pairs={{1,0},{2,1},{3,2},{4,3},{5,4},{6,5},{7,6},{8,7},{9,8},{10,9},{11,1... | collective-permute-start | bytes 9800 | tf_op jit(solution)/shard_map/ppermute | solution.py:26
  50.6 10.1 %collective-permute-start.7 = (f32[24,34,1]{2,1,0:T(8,128)S(1)}, f32[24,34,1]{2,1,0:T(8,128)S(1)}, u32[]{:S(2)}, u32[]{:S(2)}) collective-permute-start(f32[24,34,1]{2,1,0:T(8,128)S(1)} %get-tuple-element.30), channel_id=1, source_target_pairs={{0,1},{1,2},{2,3},{3,4},{4,5},{5,6},{6,7},{7,8},{8,9},{9,10},{10,1... | collective-permute-start | bytes 9800 | tf_op jit(solution)/shard_map/ppermute | solution.py:24
  62.4 7.7 %collective-permute-start.12 = (f32[16,1,256]{2,1,0:T(1,128)S(1)}, f32[16,1,256]{2,1,0:T(1,128)S(1)}, u32[]{:S(2)}, u32[]{:S(2)}) collective-permute-start(f32[16,1,256]{2,1,0:T(1,128)S(1)} %get-tuple-element.50), channel_id=1, source_target_pairs={{0,16},{16,32},{32,48},{48,64},{64,80},{80,96},{96,112},{112,128},... | collective-permute-start | bytes 49160 | tf_op jit(solution)/shard_map/ppermute | solution.py:24
  68.2 7.5 %collective-permute-start.13 = (f32[16,1,256]{2,1,0:T(1,128)S(1)}, f32[16,1,256]{2,1,0:T(1,128)S(1)}, u32[]{:S(2)}, u32[]{:S(2)}) collective-permute-start(f32[16,1,256]{2,1,0:T(1,128)S(1)} %get-tuple-element.51), channel_id=1, source_target_pairs={{16,0},{32,16},{48,32},{64,48},{80,64},{96,80},{112,96},{128,112},... | collective-permute-start | bytes 49160 | tf_op jit(solution)/shard_map/ppermute | solution.py:26
  75.9 8.4 %collective-permute-start.14 = (f32[16,34,1]{2,1,0:T(8,128)S(1)}, f32[16,34,1]{2,1,0:T(8,128)S(1)}, u32[]{:S(2)}, u32[]{:S(2)}) collective-permute-start(f32[16,34,1]{2,1,0:T(8,128)S(1)} %get-tuple-element.43), channel_id=1, source_target_pairs={{0,1},{1,2},{2,3},{3,4},{4,5},{5,6},{6,7},{7,8},{8,9},{9,10},{10,1... | collective-permute-start | bytes 6536 | tf_op jit(solution)/shard_map/ppermute | solution.py:24
  77.8 8.2 %collective-permute-start.15 = (f32[16,34,1]{2,1,0:T(8,128)S(1)}, f32[16,34,1]{2,1,0:T(8,128)S(1)}, u32[]{:S(2)}, u32[]{:S(2)}) collective-permute-start(f32[16,34,1]{2,1,0:T(8,128)S(1)} %get-tuple-element.44), channel_id=1, source_target_pairs={{1,0},{2,1},{3,2},{4,3},{5,4},{6,5},{7,6},{8,7},{9,8},{10,9},{11,1... | collective-permute-start | bytes 6536 | tf_op jit(solution)/shard_map/ppermute | solution.py:26
  88.1 5.9 %collective-permute-start.16 = (f32[24,1,256]{2,1,0:T(1,128)S(1)}, f32[24,1,256]{2,1,0:T(1,128)S(1)}, u32[]{:S(2)}, u32[]{:S(2)}) collective-permute-start(f32[24,1,256]{2,1,0:T(1,128)S(1)} %get-tuple-element.35), channel_id=1, source_target_pairs={{16,0},{32,16},{48,32},{64,48},{80,64},{96,80},{112,96},{128,112},... | collective-permute-start | bytes 73736 | tf_op jit(solution)/shard_map/ppermute | solution.py:26
  90.0 5.7 %collective-permute-start.17 = (f32[24,1,256]{2,1,0:T(1,128)S(1)}, f32[24,1,256]{2,1,0:T(1,128)S(1)}, u32[]{:S(2)}, u32[]{:S(2)}) collective-permute-start(f32[24,1,256]{2,1,0:T(1,128)S(1)} %get-tuple-element.36), channel_id=1, source_target_pairs={{0,16},{16,32},{32,48},{48,64},{64,80},{80,96},{96,112},{112,128},... | collective-permute-start | bytes 73736 | tf_op jit(solution)/shard_map/ppermute | solution.py:24
  96.9 9.3 %collective-permute-start.18 = (f32[24,34,1]{2,1,0:T(8,128)}, f32[24,34,1]{2,1,0:T(8,128)}, u32[]{:S(2)}, u32[]{:S(2)}) collective-permute-start(f32[24,34,1]{2,1,0:T(8,128)} %get-tuple-element.25), channel_id=1, source_target_pairs={{1,0},{2,1},{3,2},{4,3},{5,4},{6,5},{7,6},{8,7},{9,8},{10,9},{11,1... | collective-permute-start | bytes 9800 | tf_op jit(solution)/shard_map/ppermute | solution.py:26
  99.6 10.5 %collective-permute-start.19 = (f32[24,34,1]{2,1,0:T(8,128)}, f32[24,34,1]{2,1,0:T(8,128)}, u32[]{:S(2)}, u32[]{:S(2)}) collective-permute-start(f32[24,34,1]{2,1,0:T(8,128)} %get-tuple-element.26), channel_id=1, source_target_pairs={{0,1},{1,2},{2,3},{3,4},{4,5},{5,6},{6,7},{7,8},{8,9},{9,10},{10,1... | collective-permute-start | bytes 9800 | tf_op jit(solution)/shard_map/ppermute | solution.py:24
  337.5 5.9 %collective-permute-start.20 = (f32[16,1,256]{2,1,0:T(1,128)S(1)}, f32[16,1,256]{2,1,0:T(1,128)S(1)}, u32[]{:S(2)}, u32[]{:S(2)}) collective-permute-start(f32[16,1,256]{2,1,0:T(1,128)S(1)} %get-tuple-element.48), channel_id=1, source_target_pairs={{0,16},{16,32},{32,48},{48,64},{64,80},{80,96},{96,112},{112,128},... | collective-permute-start | bytes 49160 | tf_op jit(solution)/shard_map/ppermute | solution.py:24
  339.5 5.6 %collective-permute-start.21 = (f32[16,1,256]{2,1,0:T(1,128)S(1)}, f32[16,1,256]{2,1,0:T(1,128)S(1)}, u32[]{:S(2)}, u32[]{:S(2)}) collective-permute-start(f32[16,1,256]{2,1,0:T(1,128)S(1)} %get-tuple-element.49), channel_id=1, source_target_pairs={{16,0},{32,16},{48,32},{64,48},{80,64},{96,80},{112,96},{128,112},... | collective-permute-start | bytes 49160 | tf_op jit(solution)/shard_map/ppermute | solution.py:26
  345.3 8.4 %collective-permute-start.22 = (f32[16,34,1]{2,1,0:T(8,128)S(1)}, f32[16,34,1]{2,1,0:T(8,128)S(1)}, u32[]{:S(2)}, u32[]{:S(2)}) collective-permute-start(f32[16,34,1]{2,1,0:T(8,128)S(1)} %get-tuple-element.41), channel_id=1, source_target_pairs={{0,1},{1,2},{2,3},{3,4},{4,5},{5,6},{6,7},{7,8},{8,9},{9,10},{10,1... | collective-permute-start | bytes 6536 | tf_op jit(solution)/shard_map/ppermute | solution.py:24
  347.3 8.2 %collective-permute-start.23 = (f32[16,34,1]{2,1,0:T(8,128)S(1)}, f32[16,34,1]{2,1,0:T(8,128)S(1)}, u32[]{:S(2)}, u32[]{:S(2)}) collective-permute-start(f32[16,34,1]{2,1,0:T(8,128)S(1)} %get-tuple-element.42), channel_id=1, source_target_pairs={{1,0},{2,1},{3,2},{4,3},{5,4},{6,5},{7,6},{8,7},{9,8},{10,9},{11,1... | collective-permute-start | bytes 6536 | tf_op jit(solution)/shard_map/ppermute | solution.py:26
  356.6 5.9 %collective-permute-start.24 = (f32[24,1,256]{2,1,0:T(1,128)S(1)}, f32[24,1,256]{2,1,0:T(1,128)S(1)}, u32[]{:S(2)}, u32[]{:S(2)}) collective-permute-start(f32[24,1,256]{2,1,0:T(1,128)S(1)} %get-tuple-element.33), channel_id=1, source_target_pairs={{16,0},{32,16},{48,32},{64,48},{80,64},{96,80},{112,96},{128,112},... | collective-permute-start | bytes 73736 | tf_op jit(solution)/shard_map/ppermute | solution.py:26
  360.6 5.7 %collective-permute-start.25 = (f32[24,1,256]{2,1,0:T(1,128)S(1)}, f32[24,1,256]{2,1,0:T(1,128)S(1)}, u32[]{:S(2)}, u32[]{:S(2)}) collective-permute-start(f32[24,1,256]{2,1,0:T(1,128)S(1)} %get-tuple-element.34), channel_id=1, source_target_pairs={{0,16},{16,32},{32,48},{48,64},{64,80},{80,96},{96,112},{112,128},... | collective-permute-start | bytes 73736 | tf_op jit(solution)/shard_map/ppermute | solution.py:24
  366.6 8.7 %collective-permute-start.26 = (f32[24,34,1]{2,1,0:T(8,128)S(1)}, f32[24,34,1]{2,1,0:T(8,128)S(1)}, u32[]{:S(2)}, u32[]{:S(2)}) collective-permute-start(f32[24,34,1]{2,1,0:T(8,128)S(1)} %get-tuple-element.21), channel_id=1, source_target_pairs={{1,0},{2,1},{3,2},{4,3},{5,4},{6,5},{7,6},{8,7},{9,8},{10,9},{11,1... | collective-permute-start | bytes 9800 | tf_op jit(solution)/shard_map/ppermute | solution.py:26
  369.0 10.1 %collective-permute-start.27 = (f32[24,34,1]{2,1,0:T(8,128)S(1)}, f32[24,34,1]{2,1,0:T(8,128)S(1)}, u32[]{:S(2)}, u32[]{:S(2)}) collective-permute-start(f32[24,34,1]{2,1,0:T(8,128)S(1)} %get-tuple-element.22), channel_id=1, source_target_pairs={{0,1},{1,2},{2,3},{3,4},{4,5},{5,6},{6,7},{7,8},{8,9},{9,10},{10,1... | collective-permute-start | bytes 9800 | tf_op jit(solution)/shard_map/ppermute | solution.py:24
  380.6 107.6 %copy-start.10 = (f32[8,2,32,256]{3,2,0,1:T(8,128)S(1)}, f32[8,2,32,256]{3,2,0,1:T(8,128)}, u32[]{:S(2)}) copy-start(f32[8,2,32,256]{3,2,0,1:T(8,128)} %get-tuple-element.20) | copy-start | bytes 1572868
  380.9 107.3 %copy-start.9 = (f32[8,2,32,256]{3,2,1,0:T(8,128)S(1)}, f32[8,2,32,256]{3,2,1,0:T(8,128)}, u32[]{:S(2)}) copy-start(f32[8,2,32,256]{3,2,1,0:T(8,128)} %param.6) | copy-start | bytes 1572868
  (11 other events, 12.3 us)
